TPU v7x, 256 devices: a whole 4x4x8 slice. The times are simulated.
256 devices in a mesh: dp: 16 (over z, core), expert: 16 (over y, x).
Axes of the slice: x: 4, y: 4, z: 8, core: 2. Of those that a mesh axis runs over, the one named last changes fastest.
Arguments:
- tokens: bfloat16 [32768, 2048], P(('dp', 'expert')), may hold values from -6 to 6
- out_grad: bfloat16 [32768, 2048], P(('dp', 'expert')), may hold values from -1.5 to 1.5
- routes: int32 [32768, 2], P(('dp', 'expert')), may hold values from 0 to 15, all different within a row; in each aligned block of 128 rows (0 to 127, 128 to 255, ...) at most 32 rows name the same one
- route_probs: bfloat16 [32768, 2], P(('dp', 'expert')), may hold values from 0.049804688 to 1
- kept_count: int32 [16], P('dp'), may hold values from 512 to 2048, as said below
- gate_weight: bfloat16 [16, 2048, 768], P('expert', 'dp'), may hold values from -0.125 to 0.125
- up_weight: bfloat16 [16, 2048, 768], P('expert', 'dp'), may hold values from -0.125 to 0.125
- down_weight: bfloat16 [16, 2048, 768], P('expert', 'dp'), may hold values from -0.21875 to 0.21875
Outputs:
- token_grad: bfloat16 [32768, 2048], P(('dp', 'expert'))
- prob_grad: bfloat16 [32768, 2], P(('dp', 'expert'))
- weight_grad: bfloat16 [16, 2048, 2304], P('expert', 'dp')
Inputs may be any that keep to these rules, and one draw needn't show every extreme that they name: `routes`: among the rows of one device, no expert is named more than 32 times, and a row names 2 different experts. `kept_count`: rows of a data group whose index within the group is below its count are kept; in every draw some group keeps all its rows and another keeps a quarter of them.
All inputs are finite; a program needn't handle non-finite values.
Results may differ from a plain program's by a relative error of at most 0.018.
Values may be sent and summed in bfloat16 or wider, within the bound.
No kernel may reach another device: no remote copies, remote signals or barrier semaphores. Data moves between devices by JAX's collectives and lax.ppermute only.
A program may use at most 128 MiB of HBM per device.

v0:
```python
import jax
import jax.numpy as jnp
from jax import lax
from jax.sharding import PartitionSpec as P


def contract_rows(left, right):
    return lax.dot_general(
        left, right, (((0,), (0,)), ((), ())), preferred_element_type=jnp.float32
    )


def contract_last(left, right):
    return lax.dot_general(
        left, right, (((1,), (1,)), ((), ())), preferred_element_type=jnp.float32
    )


def per_device(
    tokens, out_grad, routes, route_probs, kept_count, gate_weight, up_weight, down_weight
):
    tok_rows, width = tokens.shape
    top = routes.shape[1]
    experts = lax.axis_size("expert")
    capacity = 2 * tok_rows * top // experts
    slots = experts * capacity
    gate_local = gate_weight[0]
    up_local = up_weight[0]
    down_local = down_weight[0]
    row = lax.axis_index("expert") * tok_rows + jnp.arange(tok_rows, dtype=jnp.int32)
    kept = row < kept_count[0]
    masked = jnp.where(kept[:, None], out_grad, jnp.zeros_like(out_grad))
    flat = routes.reshape(-1)
    onehot = (flat[:, None] == jnp.arange(experts, dtype=jnp.int32)[None, :]).astype(jnp.int32)
    before = jnp.cumsum(onehot, axis=0) - onehot
    position = jnp.sum(before * onehot, axis=1)
    target = (flat * capacity + position).reshape(tok_rows, top)
    match = target[None, :, :] == jnp.arange(slots, dtype=jnp.int32)[:, None, None]
    placing = jnp.any(match, axis=2).astype(jnp.bfloat16)
    send_rows = jnp.dot(placing, tokens, preferred_element_type=jnp.float32).astype(jnp.bfloat16)
    send_grad = jnp.dot(placing, masked, preferred_element_type=jnp.float32).astype(jnp.bfloat16)
    send_prob = jnp.sum(
        jnp.where(match, route_probs[None, :, :].astype(jnp.float32), 0.0), axis=(1, 2)
    ).astype(jnp.bfloat16)
    rows_in, grad_in, prob_in = (
        lax.all_to_all(send_rows, "expert", split_axis=0, concat_axis=0, tiled=True),
        lax.all_to_all(send_grad, "expert", split_axis=0, concat_axis=0, tiled=True),
        lax.all_to_all(send_prob, "expert", split_axis=0, concat_axis=0, tiled=True),
    )
    pieces = (
        lax.all_gather(gate_local, "dp", axis=0, tiled=True),
        lax.all_gather(up_local, "dp", axis=0, tiled=True),
    )
    pre_gate = jnp.dot(rows_in, pieces[0], preferred_element_type=jnp.float32)
    pre_up = jnp.dot(rows_in, pieces[1], preferred_element_type=jnp.float32)
    sig = jax.nn.sigmoid(pre_gate)
    act = (pre_gate * sig * pre_up).astype(jnp.bfloat16)
    scaled = (prob_in.astype(jnp.float32)[:, None] * grad_in.astype(jnp.float32)).astype(
        jnp.bfloat16
    )
    piece = lax.all_gather(down_local, "dp", axis=0, tiled=True)
    scaled_part = scaled
    output_part = contract_last(act, piece)
    back_hidden = jnp.dot(scaled_part, piece, preferred_element_type=jnp.float32)
    prob_part = jnp.sum(grad_in.astype(jnp.float32) * output_part, axis=1)
    d_gate = (back_hidden * pre_up * sig * (1.0 + pre_gate * (1.0 - sig))).astype(jnp.bfloat16)
    d_up = (back_hidden * pre_gate * sig).astype(jnp.bfloat16)
    stacked = jnp.stack((gate_local, up_local))
    pieces = lax.all_gather(stacked, "dp", axis=1, tiled=True)
    route_back = (contract_last(d_gate, pieces[0]) + contract_last(d_up, pieces[1])).astype(
        jnp.bfloat16
    )
    scaled_part = scaled
    summed = lax.psum_scatter(
        jnp.concatenate(
            (
                contract_rows(rows_in, d_gate),
                contract_rows(rows_in, d_up),
                contract_rows(scaled_part, act),
            ),
            axis=1,
        ).astype(jnp.bfloat16),
        "dp",
        scatter_dimension=0,
        tiled=True,
    )
    weight_grad = summed[None]
    rows_back, prob_back = (
        lax.all_to_all(route_back, "expert", split_axis=0, concat_axis=0, tiled=True),
        lax.all_to_all(
            prob_part.astype(jnp.bfloat16), "expert", split_axis=0, concat_axis=0, tiled=True
        ),
    )
    token_grad = contract_rows(placing, rows_back).astype(jnp.bfloat16)
    prob_grad = jnp.sum(
        jnp.where(match, prob_back.astype(jnp.float32)[:, None, None], 0.0), axis=0
    ).astype(jnp.bfloat16)
    return (token_grad, prob_grad, weight_grad)


def solution(mesh):
    in_specs = (
        P(("dp", "expert"), None),
        P(("dp", "expert"), None),
        P(("dp", "expert"), None),
        P(("dp", "expert"), None),
        P("dp"),
        P("expert", "dp", None),
        P("expert", "dp", None),
        P("expert", "dp", None),
    )
    out_specs = (P(("dp", "expert"), None), P(("dp", "expert"), None), P("expert", "dp", None))
    return jax.shard_map(
        per_device, mesh=mesh, in_specs=in_specs, out_specs=out_specs, check_vma=False
    )
```

profile of v0, /device:TPU:2, one launch (start us, length us, event | category | flops | bytes accessed | tf_op | source)
XLA Modules:
  0.0 271.1 jit_solution(16039769534471107603)
XLA Ops:
  7.2 0.7 all-gather.14.cloned.1.call-update
  8.0 0.7 all-gather.12.cloned.1.call-update
  8.7 0.7 all-gather.10.cloned.1.call-update
  9.5 1.8 pad_maximum_fusion.1
  11.3 0.8 copy.39
  12.1 0.1 eq.38
  12.2 0.1 eq.42
  12.4 0.6 reduce-window.6
  13.0 0.2 slice_reduce_fusion
  13.2 0.1 fusion.17
  13.3 0.1 reduce_sum.39
  13.5 0.1 fusion.12
  13.6 2.0 convolution_convert_fusion.3
  15.6 7.6 %all-to-all-start.2 = ((bf16[16,32,2048]{2,1,0:T(8,128)(2,1)}), bf16[16,32,2048]{2,1,0:T(8,128)(2,1)S(1)}, u32[]{:S(2)}, u32[]{:S(2)}) async-start(bf16[16,32,2048]{2,1,0:T(8,128)(2,1)} %bitcast.5), calls=%async_computation.2 | async-start | bytes 4194304 | tf_op jit(solution)/shard_map/all_to_all | solution.py:46
  23.9 2.2 convolution_convert_fusion.4
  26.1 24.3 %all-to-all-done.2 = bf16[16,32,2048]{2,1,0:T(8,128)(2,1)S(1)} async-done(((bf16[16,32,2048]{2,1,0:T(8,128)(2,1)}), bf16[16,32,2048]{2,1,0:T(8,128)(2,1)S(1)}, u32[]{:S(2)}, u32[]{:S(2)}) %all-to-all-start.2) | async-done | bytes 2097184 | tf_op jit(solution)/shard_map/all_to_all | solution.py:46
  50.4 1.3 copy-done.2
  51.7 8.1 %all-to-all-start.1 = ((bf16[16,32,2048]{2,1,0:T(8,128)(2,1)}), bf16[16,32,2048]{2,1,0:T(8,128)(2,1)S(1)}, u32[]{:S(2)}, u32[]{:S(2)}) async-start(bf16[16,32,2048]{2,1,0:T(8,128)(2,1)} %bitcast.72), calls=%async_computation.1 | async-start | bytes 4194304 | tf_op jit(solution)/shard_map/all_to_all | solution.py:47
  59.8 5.5 %fusion.4 = f32[512,768]{1,0:T(8,128)} fusion(bf16[512,2048]{1,0:T(8,128)(2,1)} %bitcast.75, bf16[1,2048,768]{2,1,0:T(8,128)(2,1)} %all-gather.14.cloned.1.call-done), kind=kOutput, calls=%fused_computation.13 | convolution fusion | flops 1610612736 | bytes 6815744 | tf_op jit(solution)/shard_map/dot_general | solution.py:54
  65.3 30.2 %all-gather.12.cloned.1.call-done = bf16[1,2048,768]{2,1,0:T(8,128)(2,1)} async-done(((bf16[1,128,768]{2,1,0:T(8,128)(2,1)}), bf16[1,2048,768]{2,1,0:T(8,128)(2,1)}) %all-gather.12.cloned.1.call-update) | async-done | bytes 3145744 | tf_op jit(solution)/shard_map/all_gather | solution.py:52
  95.5 5.9 %multiply_convert_fusion = (bf16[512,768]{1,0:T(8,128)(2,1)S(1)}, f32[512,768]{1,0:T(8,128)}) fusion(f32[512,768]{1,0:T(8,128)} %fusion.4, bf16[512,2048]{1,0:T(8,128)(2,1)} %bitcast.76, bf16[1,2048,768]{2,1,0:T(8,128)(2,1)} %all-gather.12.cloned.1.call-done), kind=kOutput, calls=%fused_computation.23 | convolution fusion | flops 1612972032 | bytes 9175040 | tf_op jit(solution)/shard_map/dot_general | solution.py:55
  101.4 35.5 %all-gather.10.cloned.1.call-done = bf16[1,2048,768]{2,1,0:T(8,128)(2,1)} async-done(((bf16[1,128,768]{2,1,0:T(8,128)(2,1)}), bf16[1,2048,768]{2,1,0:T(8,128)(2,1)}) %all-gather.10.cloned.1.call-update) | async-done | bytes 3145744 | tf_op jit(solution)/shard_map/all_gather | solution.py:61
  137.0 3.8 %fusion.1 = bf16[512]{0:T(512)(128)(2,1)S(1)} fusion(bf16[512,2048]{1,0:T(8,128)(2,1)S(1)} %bitcast.71, bf16[512,768]{1,0:T(8,128)(2,1)S(1)} %get-tuple-element.22, bf16[1,2048,768]{2,1,0:T(8,128)(2,1)} %all-gather.10.cloned.1.call-done), kind=kOutput, calls=%fused_computation.4 | convolution fusion | flops 1613757952 | bytes 6030336 | tf_op jit(solution)/shard_map/dot_general | solution.py:14
  140.8 0.7 convert_element_type.119
  141.5 7.3 %all-to-all-start.4 = ((bf16[16,32,1]{1,2,0:T(2,128)(2,1)}), bf16[16,32,1]{1,2,0:T(2,128)(2,1)S(1)}, u32[]{:S(2)}, u32[]{:S(2)}) async-start(bf16[16,32,1]{1,2,0:T(2,128)(2,1)} %convert_element_type.119), calls=%async_computation.4 | async-start | bytes 16384 | tf_op jit(solution)/shard_map/all_to_all | solution.py:90
  148.8 6.1 %all-to-all-done.4 = bf16[16,32,1]{1,2,0:T(2,128)(2,1)S(1)} async-done(((bf16[16,32,1]{1,2,0:T(2,128)(2,1)}), bf16[16,32,1]{1,2,0:T(2,128)(2,1)S(1)}, u32[]{:S(2)}, u32[]{:S(2)}) %all-to-all-start.4) | async-done | bytes 1056 | tf_op jit(solution)/shard_map/all_to_all | solution.py:90
  154.9 0.1 reshape.88
  155.0 0.7 select_reduce_fusion
  155.7 0.1 convert_element_type.118
  155.8 10.5 %all_to_all.45 = bf16[16,32,1]{1,2,0:T(2,128)(2,1)S(1)} all-to-all(bf16[16,32,1]{1,2,0:T(2,128)(2,1)S(1)} %convert_element_type.118), channel_id=1, replica_groups=mesh['dp'=16,'expert'=16] {'expert'}, dimensions={0} | all-to-all | bytes 2048 | tf_op jit(solution)/shard_map/all_to_all | solution.py:48
  166.3 0.1 reshape.86
  166.4 0.4 fusion
  166.9 1.9 convolution_convert_fusion
  168.7 0.1 copy-done.7
  168.8 0.5 copy-done.9
  169.3 0.5 copy-done.10
  169.8 2.1 multiply_convert_fusion.2
  171.9 1.9 convolution_convert_fusion.1
  173.8 1.9 convolution_convert_fusion.2
  175.7 4.5 %pad_maximum_fusion = bf16[2048,2304]{0,1:T(8,128)(2,1)} fusion(bf16[2048,768]{0,1:T(8,128)(2,1)S(1)} %convolution_convert_fusion, bf16[2048,768]{0,1:T(8,128)(2,1)S(1)} %convolution_convert_fusion.1, bf16[2048,768]{0,1:T(8,128)(2,1)S(1)} %convolution_convert_fusion.2), kind=kLoop, calls=%fused_computation | loop fusion | flops 28311552 | bytes 18874368 | tf_op jit(solution)/shard_map/concatenate | solution.py:75
  180.1 12.4 %copy.46 = bf16[2048,2304]{1,0:T(8,128)(2,1)} copy(bf16[2048,2304]{0,1:T(8,128)(2,1)} %pad_maximum_fusion) | data formatting | bytes 18874368
  192.6 3.9 %fusion.2 = f32[512,2048]{1,0:T(8,128)S(1)} fusion(bf16[512,768]{1,0:T(8,128)(2,1)S(1)} %get-tuple-element.21, bf16[2,2048,768]{2,1,0:T(8,128)(2,1)} %all-gather.8.cloned.1.call-done), kind=kOutput, calls=%fused_computation.10 | convolution fusion | flops 1610612736 | bytes 8126464 | tf_op jit(solution)/shard_map/dot_general | solution.py:14
  196.5 1.9 add_convert_fusion
  198.4 29.7 %all_to_all.46 = bf16[16,32,2048]{2,1,0:T(8,128)(2,1)S(1)} all-to-all(bf16[16,32,2048]{2,1,0:T(8,128)(2,1)S(1)} %bitcast.79), channel_id=1, replica_groups=mesh['dp'=16,'expert'=16] {'expert'}, dimensions={0} | all-to-all | bytes 4194304 | tf_op jit(solution)/shard_map/all_to_all | solution.py:89
  228.0 1.3 convolution_convert_fusion.5
  229.3 32.8 %reduce-scatter.4.cloned.1.call-done = bf16[128,2304]{1,0:T(8,128)(2,1)} async-done(((bf16[2048,2304]{1,0:T(8,128)(2,1)}), bf16[128,2304]{1,0:T(8,128)(2,1)}) %reduce-scatter.4.cloned.1.call-update) | async-done | bytes 589840
  262.1 1.4 copy.47
  263.5 1.1 copy.45
  (37 shorter events, 0.5 us)
Async XLA Ops:
  7.2 6.4 %copy-start = (bf16[128,2048]{1,0:T(8,128)(2,1)S(1)}, bf16[128,2048]{1,0:T(8,128)(2,1)}, u32[]{:S(2)}) copy-start(bf16[128,2048]{1,0:T(8,128)(2,1)} %param.8) | copy-start | bytes 1572868
  7.2 6.3 %copy-start.5 = (s32[128,2]{0,1:T(2,128)S(1)}, s32[128,2]{0,1:T(2,128)}, u32[]{:S(2)}) copy-start(s32[128,2]{0,1:T(2,128)} %param.10) | copy-start | bytes 3076
  7.2 52.6 %all-gather.14.cloned.1.call-start = ((), (), s32[]{:S(2)}) async-start(), calls=%async_computation.9 | async-start | bytes 3342336 | tf_op jit(solution)/shard_map/all_gather | solution.py:51
  7.9 87.6 %all-gather.12.cloned.1.call-start = ((), (), s32[]{:S(2)}) async-start(), calls=%async_computation.8 | async-start | bytes 3342336 | tf_op jit(solution)/shard_map/all_gather | solution.py:52
  8.7 128.3 %all-gather.10.cloned.1.call-start = ((), (), s32[]{:S(2)}) async-start(), calls=%async_computation.7 | async-start | bytes 3342336 | tf_op jit(solution)/shard_map/all_gather | solution.py:61
  9.4 183.2 %all-gather.8.cloned.1.call-start = ((), (), s32[]{:S(2)}) async-start(), calls=%async_computation.6 | async-start | bytes 6684672 | tf_op jit(solution)/shard_map/all_gather | solution.py:69
  15.6 8.3 %copy-start.4 = (bf16[128,2048]{1,0:T(8,128)(2,1)S(1)}, bf16[128,2048]{1,0:T(8,128)(2,1)}, u32[]{:S(2)}) copy-start(bf16[128,2048]{1,0:T(8,128)(2,1)} %param.9) | copy-start | bytes 1572868
  15.6 34.7 %all-to-all-start.2 = ((bf16[16,32,2048]{2,1,0:T(8,128)(2,1)}), bf16[16,32,2048]{2,1,0:T(8,128)(2,1)S(1)}, u32[]{:S(2)}, u32[]{:S(2)}) async-start(bf16[16,32,2048]{2,1,0:T(8,128)(2,1)} %bitcast.5), calls=%async_computation.2 | async-start | bytes 4194304 | tf_op jit(solution)/shard_map/all_to_all | solution.py:46
  50.4 1.3 copy-start.2
  51.7 49.8 %all-to-all-start.1 = ((bf16[16,32,2048]{2,1,0:T(8,128)(2,1)}), bf16[16,32,2048]{2,1,0:T(8,128)(2,1)S(1)}, u32[]{:S(2)}, u32[]{:S(2)}) async-start(bf16[16,32,2048]{2,1,0:T(8,128)(2,1)} %bitcast.72), calls=%async_computation.1 | async-start | bytes 4194304 | tf_op jit(solution)/shard_map/all_to_all | solution.py:47
  137.0 11.9 %copy-start.8 = (bf16[128,2]{0,1:T(2,128)(2,1)S(1)}, bf16[128,2]{0,1:T(2,128)(2,1)}, u32[]{:S(2)}) copy-start(bf16[128,2]{0,1:T(2,128)(2,1)} %param.11) | copy-start | bytes 1540
  141.5 13.4 %all-to-all-start.4 = ((bf16[16,32,1]{1,2,0:T(2,128)(2,1)}), bf16[16,32,1]{1,2,0:T(2,128)(2,1)S(1)}, u32[]{:S(2)}, u32[]{:S(2)}) async-start(bf16[16,32,1]{1,2,0:T(2,128)(2,1)} %convert_element_type.119), calls=%async_computation.4 | async-start | bytes 16384 | tf_op jit(solution)/shard_map/all_to_all | solution.py:90
  148.8 113.4 %reduce-scatter.4.cloned.1.call-start = ((), (), s32[]{:S(2)}) async-start(), calls=%async_computation.10 | async-start | bytes 10027008
  166.8 2.0 copy-start.7
  166.8 2.4 copy-start.9
  166.9 2.9 %copy-start.10 = (f32[512,768]{1,0:T(8,128)S(1)}, f32[512,768]{1,0:T(8,128)}, u32[]{:S(2)}) copy-start(f32[512,768]{1,0:T(8,128)} %get-tuple-element.23) | copy-start | bytes 4718596
  169.8 2.1 copy-start.3
  192.6 3.9 %copy-start.6 = (bf16[2,2048,768]{2,1,0:T(8,128)(2,1)S(1)}, bf16[2,2048,768]{2,1,0:T(8,128)(2,1)}, u32[]{:S(2)}) copy-start(bf16[2,2048,768]{2,1,0:T(8,128)(2,1)} %all-gather.8.cloned.1.call-done) | copy-start | bytes 18874372
  228.0 36.5 %copy-start.1 = (bf16[128,2048]{1,0:T(8,128)(2,1)S(1)}, bf16[128,2048]{1,0:T(8,128)(2,1)}, u32[]{:S(2)}) copy-start(bf16[128,2048]{1,0:T(8,128)(2,1)} %param.8) | copy-start | bytes 1572868
Sparse Core Ops, SparseCore 0:
  9.9 43.9 all-gather.13
  55.6 39.8 all-gather.11
  97.3 39.5 all-gather.9
  139.2 44.6 all-gather.7
  192.7 69.3 reduce-scatter.3
where the time goes:
time: 272 us; the launch traced here: 271 us
  waiting for transfers between devices  131 us (48%)
  blocking collectives  40.2 us (15%)
  matrix products  34.1 us (13%)
  starting transfers between devices  23.2 us (9%)
  local copies, waits for them, and re-layouts  19.7 us (7%)
  between operations  14.6 us (5%)
  other arithmetic  8.25 us (3%)
    all_gather x1, waiting for transfers between devices, per_device(): piece = lax.all_gather(down_local, 'dp', axis=0, tiled=True)  35.5 us
    unnamed x6, waiting for transfers between devices  34.9 us
    all_gather x1, waiting for transfers between devices, per_device(): lax.all_gather(up_local, 'dp', axis=0, tiled=True)  30.2 us
    all_to_all x1, blocking collectives, per_device(): lax.all_to_all(route_back, 'expert', split_axis=0, concat_axis=0, tiled=T...  29.7 us
    all_to_all x1, waiting for transfers between devices, per_device(): lax.all_to_all(send_rows, 'expert', split_axis=0, concat_axis=0, tiled=True)  24.3 us
    unnamed x26, local copies, waits for them, and re-layouts  18.1 us
    all_to_all x1, blocking collectives, per_device(): lax.all_to_all(send_prob, 'expert', split_axis=0, concat_axis=0, tiled=True)  10.5 us
    dot_general x3, matrix products, contract_last(): lax.dot_general(left, right, (((1,), (1,)), ((), ())), preferred_element_...  9.55 us
  transfers between devices with their start and end apart: 8, of which 5 were waited for; matrix products, arithmetic and copies ran while one was open for 21% of the time, Pallas kernels for 0%

commit v1 on v0

--- a/solution.py
+++ b/solution.py
@@ -2,6 +2,10 @@
 import jax.numpy as jnp
 from jax import lax
 from jax.sharding import PartitionSpec as P
+
+lay_plate = lambda piece_in: jnp.concatenate(
+    lax.all_to_all(jnp.stack(lax.axis_size("dp") * [piece_in]), "dp", 0, 0), axis=0
+)
 
 
 def contract_rows(left, right):
@@ -58,7 +62,7 @@
     scaled = (prob_in.astype(jnp.float32)[:, None] * grad_in.astype(jnp.float32)).astype(
         jnp.bfloat16
     )
-    piece = lax.all_gather(down_local, "dp", axis=0, tiled=True)
+    piece = lay_plate(down_local)
     scaled_part = scaled
     output_part = contract_last(act, piece)
     back_hidden = jnp.dot(scaled_part, piece, preferred_element_type=jnp.float32)

time: 272 us -> 333 us (1.22)
  waiting for transfers between devices: 131 us -> 177 us
  starting transfers between devices: 23.2 us -> 31.9 us
  local copies, waits for them, and re-layouts: 19.7 us -> 23.1 us
    all_to_all x0 -> x1, waiting for transfers between devices: none -> 85.3 us  [lax.all_to_all(jnp.stack(lax.axis_size('dp') * [piece_in]), 'dp', 0, 0)]
    all_gather x1 -> x0, waiting for transfers between devices: 35.5 us -> none  [per_device(): piece = lax.all_gather(down_local, 'dp', axis=0, tiled=True)]
    all_gather x1, waiting for transfers between devices: 30.2 us -> 0.01 us  [per_device(): lax.all_gather(up_local, 'dp', axis=0, tiled=True)]
    all_to_all x1, waiting for transfers between devices: 0.01 us -> 25.8 us  [per_device(): lax.all_to_all(send_grad, 'expert', split_axis=0, concat_axis=0, tiled=True)]
    all_to_all x0 -> x1, starting transfers between devices: none -> 8.61 us  [lax.all_to_all(jnp.stack(lax.axis_size('dp') * [piece_in]), 'dp', 0, 0)]
    unnamed x26 -> x30, local copies, waits for them, and re-layouts: 18.1 us -> 19.6 us
    unnamed x6 -> x5, waiting for transfers between devices: 34.9 us -> 35.2 us
  transfers between devices with their start and end apart: 8 -> 8, of which waited for: 5 -> 5; matrix products, arithmetic and copies ran while one was open for 21% -> 19% of each run, Pallas kernels for 0% -> 0%
where the time goes in v1:
time: 333 us
  waiting for transfers between devices  177 us (53%)
  blocking collectives  41 us (12%)
  matrix products  36.7 us (11%)
  starting transfers between devices  31.9 us (10%)
  local copies, waits for them, and re-layouts  23.1 us (7%)
  between operations  14.7 us (4%)
  other arithmetic  8.27 us (2%)
    all_to_all x1, waiting for transfers between devices, lax.all_to_all(jnp.stack(lax.axis_size('dp') * [piece_in]), 'dp', 0, 0)  85.3 us
    unnamed x5, waiting for transfers between devices  35.2 us
    all_to_all x1, blocking collectives, per_device(): lax.all_to_all(route_back, 'expert', split_axis=0, concat_axis=0, tiled=T...  30.5 us
    all_to_all x1, waiting for transfers between devices, per_device(): lax.all_to_all(send_grad, 'expert', split_axis=0, concat_axis=0, tiled=True)  25.8 us
    all_to_all x1, waiting for transfers between devices, per_device(): lax.all_to_all(send_rows, 'expert', split_axis=0, concat_axis=0, tiled=True)  24.4 us
    unnamed x30, local copies, waits for them, and re-layouts  19.6 us
    all_to_all x1, blocking collectives, per_device(): lax.all_to_all(send_prob, 'expert', split_axis=0, concat_axis=0, tiled=True)  10.6 us
    dot_general x3, matrix products, contract_last(): lax.dot_general(left, right, (((1,), (1,)), ((), ())), preferred_element_...  9.84 us
  transfers between devices with their start and end apart: 8, of which 5 were waited for; matrix products, arithmetic and copies ran while one was open for 19% of the time, Pallas kernels for 0%

profile of v1, /device:TPU:2, one launch (start us, length us, event | category | flops | bytes accessed | tf_op | source)
XLA Modules:
  0.0 332.5 jit_solution(16969919124670220430)
XLA Ops:
  7.2 0.7 all-gather.10.cloned.1.call-update
  8.0 0.7 all-gather.8.cloned.1.call-update
  8.7 0.8 copy.47
  9.5 0.1 eq.38
  9.6 0.1 eq.42
  9.7 0.6 reduce-window.6
  10.3 0.2 slice_reduce_fusion
  10.6 0.1 fusion.15
  10.7 0.1 reduce_sum.39
  10.9 0.7 multiply_add_fusion
  11.6 2.0 convolution_convert_fusion.3
  13.7 7.6 %all-to-all-start.3 = ((bf16[16,32,2048]{2,1,0:T(8,128)(2,1)}), bf16[16,32,2048]{2,1,0:T(8,128)(2,1)S(1)}, u32[]{:S(2)}, u32[]{:S(2)}) async-start(bf16[16,32,2048]{2,1,0:T(8,128)(2,1)} %bitcast.7), calls=%async_computation.3 | async-start | bytes 4194304 | tf_op jit(solution)/shard_map/all_to_all | solution.py:50
  22.0 2.1 convolution_convert_fusion.4
  24.1 24.4 %all-to-all-done.3 = bf16[16,32,2048]{2,1,0:T(8,128)(2,1)S(1)} async-done(((bf16[16,32,2048]{2,1,0:T(8,128)(2,1)}), bf16[16,32,2048]{2,1,0:T(8,128)(2,1)S(1)}, u32[]{:S(2)}, u32[]{:S(2)}) %all-to-all-start.3) | async-done | bytes 2097184 | tf_op jit(solution)/shard_map/all_to_all | solution.py:50
  48.4 1.3 copy-done.2
  49.8 8.1 %all-to-all-start.1 = ((bf16[16,32,2048]{2,1,0:T(8,128)(2,1)}), bf16[16,32,2048]{2,1,0:T(8,128)(2,1)S(1)}, u32[]{:S(2)}, u32[]{:S(2)}) async-start(bf16[16,32,2048]{2,1,0:T(8,128)(2,1)} %bitcast.74), calls=%async_computation.1 | async-start | bytes 4194304 | tf_op jit(solution)/shard_map/all_to_all | solution.py:51
  58.0 0.8 pad_maximum_fusion.1
  58.8 25.8 %all-to-all-done.1 = bf16[16,32,2048]{2,1,0:T(8,128)(2,1)S(1)} async-done(((bf16[16,32,2048]{2,1,0:T(8,128)(2,1)}), bf16[16,32,2048]{2,1,0:T(8,128)(2,1)S(1)}, u32[]{:S(2)}, u32[]{:S(2)}) %all-to-all-start.1) | async-done | bytes 2097184 | tf_op jit(solution)/shard_map/all_to_all | solution.py:51
  84.5 1.9 stack.6
  86.5 8.6 %all-to-all-start.2 = ((bf16[16,128,768]{2,1,0:T(8,128)(2,1)}), bf16[16,128,768]{2,1,0:T(8,128)(2,1)}, u32[]{:S(2)}, u32[]{:S(2)}) async-start(bf16[16,128,768]{2,1,0:T(8,128)(2,1)} %stack.6), calls=%async_computation.2 | async-start | bytes 6291456 | tf_op jit(solution)/shard_map/all_to_all | solution.py:7
  95.1 5.5 %fusion.5 = f32[512,768]{1,0:T(8,128)} fusion(bf16[512,2048]{1,0:T(8,128)(2,1)} %bitcast.77, bf16[1,2048,768]{2,1,0:T(8,128)(2,1)} %all-gather.10.cloned.1.call-done), kind=kOutput, calls=%fused_computation.15 | convolution fusion | flops 1610612736 | bytes 6815744 | tf_op jit(solution)/shard_map/dot_general | solution.py:58
  100.6 6.2 %multiply_convert_fusion = (bf16[512,768]{1,0:T(8,128)(2,1)}, f32[512,768]{1,0:T(8,128)}) fusion(f32[512,768]{1,0:T(8,128)} %fusion.5, bf16[512,2048]{1,0:T(8,128)(2,1)} %bitcast.78, bf16[1,2048,768]{2,1,0:T(8,128)(2,1)} %all-gather.8.cloned.1.call-done), kind=kOutput, calls=%fused_computation.22 | convolution fusion | flops 1612972032 | bytes 9175040 | tf_op jit(solution)/shard_map/dot_general | solution.py:59
  106.8 85.3 %all-to-all-done.2 = bf16[16,128,768]{2,1,0:T(8,128)(2,1)} async-done(((bf16[16,128,768]{2,1,0:T(8,128)(2,1)}), bf16[16,128,768]{2,1,0:T(8,128)(2,1)}, u32[]{:S(2)}, u32[]{:S(2)}) %all-to-all-start.2) | async-done | bytes 3145760 | tf_op jit(solution)/shard_map/all_to_all | solution.py:7
  192.1 4.1 %fusion.1 = bf16[512]{0:T(512)(128)(2,1)S(1)} fusion(bf16[16,32,2048]{2,1,0:T(8,128)(2,1)S(1)} %all-to-all-done.1, bf16[512,768]{1,0:T(8,128)(2,1)} %get-tuple-element.25, bf16[2048,768]{1,0:T(8,128)(2,1)} %bitcast.6), kind=kOutput, calls=%fused_computation.5 | convolution fusion | flops 1613757952 | bytes 6030336 | tf_op jit(solution)/shard_map/dot_general | solution.py:18
  196.3 0.7 convert_element_type.139
  196.9 7.4 %all-to-all-start.5 = ((bf16[16,32,1]{1,2,0:T(2,128)(2,1)}), bf16[16,32,1]{1,2,0:T(2,128)(2,1)S(1)}, u32[]{:S(2)}, u32[]{:S(2)}) async-start(bf16[16,32,1]{1,2,0:T(2,128)(2,1)} %convert_element_type.139), calls=%async_computation.5 | async-start | bytes 16384 | tf_op jit(solution)/shard_map/all_to_all | solution.py:94
  204.4 6.1 %all-to-all-done.5 = bf16[16,32,1]{1,2,0:T(2,128)(2,1)S(1)} async-done(((bf16[16,32,1]{1,2,0:T(2,128)(2,1)}), bf16[16,32,1]{1,2,0:T(2,128)(2,1)S(1)}, u32[]{:S(2)}, u32[]{:S(2)}) %all-to-all-start.5) | async-done | bytes 1056 | tf_op jit(solution)/shard_map/all_to_all | solution.py:94
  210.6 0.7 select_reduce_fusion
  211.3 0.1 convert_element_type.138
  211.4 10.6 %all_to_all.50 = bf16[16,32,1]{1,2,0:T(2,128)(2,1)S(1)} all-to-all(bf16[16,32,1]{1,2,0:T(2,128)(2,1)S(1)} %convert_element_type.138), channel_id=1, replica_groups=mesh['dp'=16,'expert'=16] {'expert'}, dimensions={0} | all-to-all | bytes 2048 | tf_op jit(solution)/shard_map/all_to_all | solution.py:52
  222.1 0.4 fusion.2
  222.5 0.7 copy-done.11
  223.2 1.9 convolution_convert_fusion
  225.1 0.4 fusion
  225.5 1.0 copy-done.10
  226.5 0.5 copy-done.12
  227.0 4.2 %multiply_convert_fusion.2 = (bf16[512,768]{1,0:T(8,128)(2,1)S(1)}, bf16[512,768]{1,0:T(8,128)(2,1)S(1)}) fusion(f32[512,768]{1,0:T(8,128)S(1)} %copy-done.10, f32[512,768]{1,0:T(8,128)S(1)} %copy-done.12, bf16[512,2048]{1,0:T(8,128)(2,1)S(1)} %bitcast.81, bf16[2048,768]{1,0:T(8,128)(2,1)} %bitcast.6), kind=kOutput, calls=%fused_computation.24 | convolution fusion | flops 1615724544 | bytes 9961472 | tf_op jit(solution)/shard_map/dot_general | solution.py:68
  231.2 1.9 convolution_convert_fusion.1
  233.0 1.9 convolution_convert_fusion.2
  234.9 4.4 %pad_maximum_fusion = bf16[2048,2304]{0,1:T(8,128)(2,1)} fusion(bf16[2048,768]{0,1:T(8,128)(2,1)S(1)} %convolution_convert_fusion, bf16[2048,768]{0,1:T(8,128)(2,1)S(1)} %convolution_convert_fusion.1, bf16[2048,768]{0,1:T(8,128)(2,1)S(1)} %convolution_convert_fusion.2), kind=kLoop, calls=%fused_computation | loop fusion | flops 28311552 | bytes 18874368 | tf_op jit(solution)/shard_map/concatenate | solution.py:79
  239.4 12.8 %copy.54 = bf16[2048,2304]{1,0:T(8,128)(2,1)} copy(bf16[2048,2304]{0,1:T(8,128)(2,1)} %pad_maximum_fusion) | data formatting | bytes 18874368
  252.2 3.9 %fusion.3 = f32[512,2048]{1,0:T(8,128)S(1)} fusion(bf16[512,768]{1,0:T(8,128)(2,1)S(1)} %get-tuple-element.24, bf16[2,2048,768]{2,1,0:T(8,128)(2,1)} %all-gather.6.cloned.1.call-done), kind=kOutput, calls=%fused_computation.12 | convolution fusion | flops 1610612736 | bytes 8126464 | tf_op jit(solution)/shard_map/dot_general | solution.py:18
  256.1 1.9 add_convert_fusion
  258.0 30.5 %all_to_all.51 = bf16[16,32,2048]{2,1,0:T(8,128)(2,1)S(1)} all-to-all(bf16[16,32,2048]{2,1,0:T(8,128)(2,1)S(1)} %bitcast.82), channel_id=1, replica_groups=mesh['dp'=16,'expert'=16] {'expert'}, dimensions={0} | all-to-all | bytes 4194304 | tf_op jit(solution)/shard_map/all_to_all | solution.py:93
  288.4 1.3 convolution_convert_fusion.5
  289.7 33.8 %reduce-scatter.4.cloned.1.call-done = bf16[128,2304]{1,0:T(8,128)(2,1)} async-done(((bf16[2048,2304]{1,0:T(8,128)(2,1)}), bf16[128,2304]{1,0:T(8,128)(2,1)}) %reduce-scatter.4.cloned.1.call-update) | async-done | bytes 589840
  323.5 1.4 copy.55
  324.9 1.1 copy.53
  (43 shorter events, 0.7 us)
Async XLA Ops:
  7.2 4.5 %copy-start = (bf16[128,2048]{1,0:T(8,128)(2,1)S(1)}, bf16[128,2048]{1,0:T(8,128)(2,1)}, u32[]{:S(2)}) copy-start(bf16[128,2048]{1,0:T(8,128)(2,1)} %param.8) | copy-start | bytes 1572868
  7.2 87.9 %all-gather.10.cloned.1.call-start = ((), (), s32[]{:S(2)}) async-start(), calls=%async_computation.9 | async-start | bytes 3342336 | tf_op jit(solution)/shard_map/all_gather | solution.py:55
  7.9 92.7 %all-gather.8.cloned.1.call-start = ((), (), s32[]{:S(2)}) async-start(), calls=%async_computation.8 | async-start | bytes 3342336 | tf_op jit(solution)/shard_map/all_gather | solution.py:56
  13.7 8.3 %copy-start.6 = (bf16[128,2048]{1,0:T(8,128)(2,1)S(1)}, bf16[128,2048]{1,0:T(8,128)(2,1)}, u32[]{:S(2)}) copy-start(bf16[128,2048]{1,0:T(8,128)(2,1)} %param.9) | copy-start | bytes 1572868
  13.7 34.7 %all-to-all-start.3 = ((bf16[16,32,2048]{2,1,0:T(8,128)(2,1)}), bf16[16,32,2048]{2,1,0:T(8,128)(2,1)S(1)}, u32[]{:S(2)}, u32[]{:S(2)}) async-start(bf16[16,32,2048]{2,1,0:T(8,128)(2,1)} %bitcast.7), calls=%async_computation.3 | async-start | bytes 4194304 | tf_op jit(solution)/shard_map/all_to_all | solution.py:50
  48.4 1.3 copy-start.2
  48.4 9.5 %copy-start.4 = (bf16[1,128,768]{2,1,0:T(8,128)(2,1)S(1)}, bf16[1,128,768]{2,1,0:T(8,128)(2,1)}, u32[]{:S(2)}) copy-start(bf16[1,128,768]{2,1,0:T(8,128)(2,1)} %param.13) | copy-start | bytes 589828
  48.4 9.5 %copy-start.5 = (bf16[1,128,768]{2,1,0:T(8,128)(2,1)S(1)}, bf16[1,128,768]{2,1,0:T(8,128)(2,1)}, u32[]{:S(2)}) copy-start(bf16[1,128,768]{2,1,0:T(8,128)(2,1)} %param.14) | copy-start | bytes 589828
  48.4 36.1 %copy-start.7 = (bf16[1,128,768]{2,1,0:T(8,128)(2,1)S(1)}, bf16[1,128,768]{2,1,0:T(8,128)(2,1)}, u32[]{:S(2)}) copy-start(bf16[1,128,768]{2,1,0:T(8,128)(2,1)} %param.15) | copy-start | bytes 589828
  49.8 34.8 %all-to-all-start.1 = ((bf16[16,32,2048]{2,1,0:T(8,128)(2,1)}), bf16[16,32,2048]{2,1,0:T(8,128)(2,1)S(1)}, u32[]{:S(2)}, u32[]{:S(2)}) async-start(bf16[16,32,2048]{2,1,0:T(8,128)(2,1)} %bitcast.74), calls=%async_computation.1 | async-start | bytes 4194304 | tf_op jit(solution)/shard_map/all_to_all | solution.py:51
  57.9 194.3 %all-gather.6.cloned.1.call-start = ((), (), s32[]{:S(2)}) async-start(), calls=%async_computation.7 | async-start | bytes 6684672 | tf_op jit(solution)/shard_map/all_gather | solution.py:73
  86.5 105.6 %all-to-all-start.2 = ((bf16[16,128,768]{2,1,0:T(8,128)(2,1)}), bf16[16,128,768]{2,1,0:T(8,128)(2,1)}, u32[]{:S(2)}, u32[]{:S(2)}) async-start(bf16[16,128,768]{2,1,0:T(8,128)(2,1)} %stack.6), calls=%async_computation.2 | async-start | bytes 6291456 | tf_op jit(solution)/shard_map/all_to_all | solution.py:7
  192.1 12.2 %copy-start.9 = (bf16[128,2]{0,1:T(2,128)(2,1)S(1)}, bf16[128,2]{0,1:T(2,128)(2,1)}, u32[]{:S(2)}) copy-start(bf16[128,2]{0,1:T(2,128)(2,1)} %param.11) | copy-start | bytes 1540
  196.9 13.6 %all-to-all-start.5 = ((bf16[16,32,1]{1,2,0:T(2,128)(2,1)}), bf16[16,32,1]{1,2,0:T(2,128)(2,1)S(1)}, u32[]{:S(2)}, u32[]{:S(2)}) async-start(bf16[16,32,1]{1,2,0:T(2,128)(2,1)} %convert_element_type.139), calls=%async_computation.5 | async-start | bytes 16384 | tf_op jit(solution)/shard_map/all_to_all | solution.py:94
  204.3 119.2 %reduce-scatter.4.cloned.1.call-start = ((), (), s32[]{:S(2)}) async-start(), calls=%async_computation.10 | async-start | bytes 10027008
  222.1 1.1 copy-start.11
  225.1 1.4 copy-start.10
  225.1 1.9 copy-start.12
  227.0 4.2 %copy-start.3 = (bf16[16,32,2048]{2,1,0:T(8,128)(2,1)S(1)}, bf16[16,32,2048]{2,1,0:T(8,128)(2,1)}, u32[]{:S(2)}) copy-start(bf16[16,32,2048]{2,1,0:T(8,128)(2,1)} %copy-done.2) | copy-start | bytes 6291460
  252.2 3.9 %copy-start.8 = (bf16[2,2048,768]{2,1,0:T(8,128)(2,1)S(1)}, bf16[2,2048,768]{2,1,0:T(8,128)(2,1)}, u32[]{:S(2)}) copy-start(bf16[2,2048,768]{2,1,0:T(8,128)(2,1)} %all-gather.6.cloned.1.call-done) | copy-start | bytes 18874372
  288.4 37.5 %copy-start.1 = (bf16[128,2048]{1,0:T(8,128)(2,1)S(1)}, bf16[128,2048]{1,0:T(8,128)(2,1)}, u32[]{:S(2)}) copy-start(bf16[128,2048]{1,0:T(8,128)(2,1)} %param.8) | copy-start | bytes 1572868
Sparse Core Ops, SparseCore 0:
  9.8 44.0 all-gather.9
  55.7 39.6 all-gather.7
  97.9 100.0 all-gather.5
  252.3 71.1 reduce-scatter.3
